TPU v7x, 32 devices: a whole 2x2x4 slice. The times are simulated.
32 devices in a mesh: rep: 2 (over y), ctx: 4 (over z), ch: 2 (over x), sub: 2 (over core).
Axes of the slice: x: 2, y: 2, z: 4, core: 2. Of those that a mesh axis runs over, the one named last changes fastest.
Arguments:
- hyena_query: bfloat16 [3072, 8192], P(('rep', 'ctx'), ('ch', 'sub')), parts along dimension 0, may hold values from -6 to 6
- hyena_key: bfloat16 [3072, 8192], P(('rep', 'ctx'), ('ch', 'sub')), parts along dimension 0, may hold values from -6 to 6
- hyena_value: bfloat16 [3072, 8192], P(('rep', 'ctx'), ('ch', 'sub')), parts along dimension 0, may hold values from -6 to 6
- filters: bfloat16 [512, 128], P(('ch', 'sub')), may hold values from -0.5 to 0.5
- skip_gain: float32 [8192], P(('ch', 'sub')), may hold values from 0.5 to 1.5
- attn_query: bfloat16 [3072, 8192], P(('rep', 'ctx'), ('ch', 'sub')), parts along dimension 0, may hold values from -40 to 40
- attn_key: bfloat16 [3072, 8192], P(('rep', 'ctx'), ('ch', 'sub')), parts along dimension 0, may hold values from -5 to 5
- genome_starts: int32 [8], P('rep'), parts along dimension 0, may hold values from 0 to 1408, as said below
Outputs:
- hyena_mix: bfloat16 [3072, 8192], P(('rep', 'ctx'), ('ch', 'sub')), parts along dimension 0
- attended: bfloat16 [3072, 8192], P(('rep', 'ctx'), ('ch', 'sub')), parts along dimension 0
There are 2 independent parts, one for each index of `rep`. A program takes and returns all parts, laid end to end along the dimension named above; an argument that names none is the same for every part. Nothing has to cross between parts.
Inputs may be any that keep to these rules, and one draw needn't show every extreme that they name: genome_starts[0] is 0; the entries rise, each by 128 or more, and the last genome holds exactly 128 positions.
All inputs are finite; a program needn't handle non-finite values.
Results may differ from a plain program's by a relative error of at most 0.0059.
Values may be sent and summed in bfloat16 or wider, within the bound.
A program may use at most 128 MiB of HBM per device.

v0:
```python
from functools import partial
import math
import jax
import jax.numpy as jnp
from jax import lax
from jax.sharding import PartitionSpec as P

HEAD_DIM = 128


def passed_along(value, axis, by):
    devices = lax.axis_size(axis)
    pairs = [(i, i + by) for i in range(devices) if 0 <= i + by < devices]
    return lax.ppermute(value, axis, pairs)


def genome_index(positions, genome_starts):
    inside = genome_starts[None, :] <= positions[:, None]
    return jnp.sum(inside.astype(jnp.int32), axis=1) - 1


def genome_begin(positions, genome_starts):
    inside = genome_starts[None, :] <= positions[:, None]
    return jnp.max(jnp.where(inside, genome_starts[None, :], 0), axis=1)


def grouped_filter(product, parity, filters, left_pad):
    channels = product.shape[1]
    group_width = channels // filters.shape[0]
    kernel = jnp.repeat(filters, group_width, axis=0).T[::-1][:, None, :]
    nothing = jnp.zeros_like(product)
    even_rows = jnp.where((parity == 0)[:, None], product, nothing)
    odd_rows = jnp.where((parity == 1)[:, None], product, nothing)
    stacked = jnp.stack([even_rows, odd_rows])
    return lax.conv_general_dilated(
        stacked,
        kernel,
        (1,),
        [(left_pad, 0)],
        dimension_numbers=("NWC", "WIO", "NWC"),
        feature_group_count=channels,
        preferred_element_type=jnp.float32,
    )


def attend_update(carried, queries, query_pos, query_begin, key_heads, value_heads, key_pos):
    weighted, running_max, weight_sum = carried
    score_scale = 1.0 / math.sqrt(HEAD_DIM)
    scores = (
        jnp.einsum("qhd,khd->hqk", queries, key_heads, preferred_element_type=jnp.float32)
        * score_scale
    )
    visible = (key_pos[None, :] <= query_pos[:, None]) & (key_pos[None, :] >= query_begin[:, None])
    new_max = jnp.maximum(running_max, jnp.max(jnp.where(visible[None], scores, -1e30), axis=2))
    weights = jnp.exp(jnp.where(visible[None], scores - new_max[:, :, None], -1e30))
    mixed = jnp.einsum(
        "hqk,khd->hqd",
        weights.astype(jnp.bfloat16),
        value_heads,
        preferred_element_type=jnp.float32,
    )
    return (mixed, new_max, jnp.sum(weights, axis=2))


def keep_state(carried):
    return carried


def per_device(
    hyena_query, hyena_key, hyena_value, filters, skip_gain, attn_query, attn_key, genome_starts
):
    local_rows, channels = hyena_key.shape
    taps = filters.shape[1]
    shard_first = lax.axis_index("ctx") * local_rows
    product = lax.optimization_barrier(
        (hyena_key.astype(jnp.float32) * hyena_value.astype(jnp.float32)).astype(jnp.bfloat16)
    )
    earlier = passed_along(product[local_rows - (taps - 1) :], "ctx", 1)
    extended = jnp.concatenate([earlier, product], axis=0)
    extended_pos = shard_first - (taps - 1) + jnp.arange(local_rows + taps - 1, dtype=jnp.int32)
    both_parities = grouped_filter(
        extended, genome_index(extended_pos, genome_starts) % 2, filters, 0
    )
    own_pos = shard_first + jnp.arange(local_rows, dtype=jnp.int32)
    own_parity = genome_index(own_pos, genome_starts) % 2
    filtered = jnp.where((own_parity == 0)[:, None], both_parities[0], both_parities[1])
    hyena_mix = (
        hyena_query.astype(jnp.float32)
        * (filtered + skip_gain[None, :] * product.astype(jnp.float32))
    ).astype(jnp.bfloat16)
    head_count = channels // HEAD_DIM
    queries = attn_query.reshape(local_rows, head_count, HEAD_DIM)
    pairs = [(queries, own_pos)]
    groups = [
        (group_queries, group_pos, genome_begin(group_pos, genome_starts))
        for group_queries, group_pos in pairs
    ]
    initial = tuple(
        (
            (
                jnp.zeros((head_count, group_pos.shape[0], HEAD_DIM), jnp.float32),
                jnp.full((head_count, group_pos.shape[0]), -1e30, jnp.float32),
                jnp.zeros((head_count, group_pos.shape[0]), jnp.float32),
            )
            for group_queries, group_pos, group_begin in groups
        )
    )
    offset_row = jnp.int32(0)
    keys_piece = lax.all_gather(attn_key, "ctx", axis=0, tiled=True)
    values_piece = lax.all_gather(hyena_mix, "ctx", axis=0, tiled=True)
    key_rows = keys_piece.shape[0]
    key_heads = keys_piece.reshape(key_rows, head_count, HEAD_DIM)
    value_heads = values_piece.reshape(key_rows, head_count, HEAD_DIM)
    key_pos = jnp.arange(key_rows, dtype=jnp.int32)
    updated = []
    for state_now, (group_queries, group_pos, group_begin) in zip(initial, groups):
        needed = (offset_row <= jnp.max(group_pos)) & (offset_row + key_rows > jnp.min(group_begin))
        update = partial(
            attend_update,
            queries=group_queries,
            query_pos=group_pos,
            query_begin=group_begin,
            key_heads=key_heads,
            value_heads=value_heads,
            key_pos=key_pos,
        )
        updated.append(lax.cond(needed, update, keep_state, state_now))
    results = tuple(updated)
    outputs = []
    for weighted, running_max, weight_sum in results:
        finished = (weighted / weight_sum[:, :, None]).astype(jnp.bfloat16)
        outputs.append(finished.transpose(1, 0, 2).reshape(weighted.shape[1], channels))
    attended = outputs[0]
    return (hyena_mix, attended)


def solution(mesh):
    return jax.shard_map(
        per_device,
        mesh=mesh,
        in_specs=(
            P(("rep", "ctx"), ("ch", "sub")),
            P(("rep", "ctx"), ("ch", "sub")),
            P(("rep", "ctx"), ("ch", "sub")),
            P(("ch", "sub"), None),
            P(("ch", "sub")),
            P(("rep", "ctx"), ("ch", "sub")),
            P(("rep", "ctx"), ("ch", "sub")),
            P("rep"),
        ),
        out_specs=(P(("rep", "ctx"), ("ch", "sub")), P(("rep", "ctx"), ("ch", "sub"))),
        check_vma=False,
    )
```

profile of v0, /device:TPU:0, one launch (start us, length us, event | category | flops | bytes accessed | tf_op | source)
XLA Modules:
  0.0 359.8 jit_solution(4277070580375410780)
XLA Ops:
  7.2 0.0 all-gather.3.cloned.1.call-start
  7.2 0.7 all-gather.3.cloned.1.call-update
  7.9 0.0 all-gather.5.cloned.1.call-start
  8.0 2.5 multiply_convert_fusion
  10.5 1.0 slice.12
  11.5 5.7 %collective-permute-start = (bf16[127,2048]{1,0:T(8,128)(2,1)}, bf16[127,2048]{1,0:T(8,128)(2,1)}, u32[]{:S(2)}, u32[]{:S(2)}) collective-permute-start(bf16[127,2048]{1,0:T(8,128)(2,1)} %slice.12), channel_id=1, source_target_pairs={{0,4},{4,8},{8,12},{1,5},{5,9},{9,13},{2,6},{6,10},{10,14},{3,7},{... | collective-permute-start | bytes 1560584 | tf_op jit(solution)/shard_map/ppermute | solution.py:14
  17.2 0.1 convert_reduce_fusion
  17.3 0.1 broadcast_in_dim.88
  17.4 1.5 rev.3
  18.9 0.9 copy.43
  19.8 0.7 fusion.24
  20.5 0.5 fusion.26
  21.1 13.9 %collective-permute-done = bf16[127,2048]{1,0:T(8,128)(2,1)} collective-permute-done((bf16[127,2048]{1,0:T(8,128)(2,1)}, bf16[127,2048]{1,0:T(8,128)(2,1)}, u32[]{:S(2)}, u32[]{:S(2)}) %collective-permute-start) | collective-permute-done | bytes 520224 | tf_op jit(solution)/shard_map/ppermute | solution.py:14
  34.9 1.9 copy_dynamic-update-slice_fusion.1
  36.8 2.6 copy_dynamic-update-slice_fusion
  39.4 8.6 %broadcast_select_fusion.1 = (bf16[1,511,2048]{2,0,1:T(2,128)(2,1)S(1)}, bf16[1,511,2048]{2,0,1:T(2,128)(2,1)S(1)}) fusion(bf16[1,511,2048]{2,0,1:T(2,128)(2,1)S(1)} %copy_dynamic-update-slice_fusion, pred[511]{0:T(512)(128)(4,1)S(1)} %get-tuple-element.33, pred[511]{0:T(512)(128)(4,1)S(1)} %broadcast_compare_fusion), kind=kLoop, calls=%fused_computation.18 | loop fusion | flops 2093056 | bytes 6280190 | tf_op jit(solution)/shard_map/jit(_where)/select_n | solution.py:32
  48.1 9.6 %fusion.39 = bf16[2,511,2048]{2,0,1:T(2,128)(2,1)S(1)} fusion(bf16[1,511,2048]{2,0,1:T(2,128)(2,1)S(1)} %get-tuple-element.40, bf16[1,511,2048]{2,0,1:T(2,128)(2,1)S(1)} %get-tuple-element.39), kind=kLoop, calls=%fused_computation.20.clone.1 | loop fusion | flops 8372224 | bytes 8372224 | tf_op jit(solution)/shard_map/conv_general_dilated | solution.py:35
  57.7 90.8 %fusion.14 = f32[2,384,2048]{2,0,1:T(2,128)} fusion(bf16[128,1,2048]{2,1,0:T(2,128)(2,1)S(1)} %copy.43, bf16[2,511,2048]{2,0,1:T(2,128)(2,1)S(1)} %fusion.39), kind=kOutput, calls=%fused_computation.19 | convolution fusion | flops 402653184 | bytes 11001856 | tf_op jit(solution)/shard_map/conv_general_dilated | solution.py:35
  148.5 13.9 %fusion.30 = (f32[1,384,2048]{2,0,1:T(1,128)}, f32[1,384,2048]{2,0,1:T(1,128)}) fusion(f32[2,384,2048]{2,0,1:T(2,128)} %fusion.14), kind=kLoop, calls=%fused_computation.54 | loop fusion | bytes 12582912 | tf_op jit(solution)/shard_map/slice | solution.py:86
  162.5 6.9 %fusion.21 = bf16[384,2048]{1,0:T(8,128)(2,1)} fusion(f32[1,384,2048]{2,0,1:T(1,128)} %get-tuple-element.38, f32[1,384,2048]{2,0,1:T(1,128)} %get-tuple-element.37, bf16[384,2048]{1,0:T(8,128)(2,1)S(1)} %copy-done.1, bf16[384,2048]{1,0:T(8,128)(2,1)S(1)} %copy-done.4, f32[2048]{0:T(1024)S(1)} %copy-done.9, pred[384]{0:T(512)(128)(4,1)S(1)} %copy-done.10), kind=kLoop, calls=%fused_computation.27 | loop fusion | flops 5505024 | bytes 11018624 | tf_op jit(solution)/shard_map/convert_element_type | solution.py:90
  169.4 0.0 all-gather.5.cloned.1.call-update
  169.4 0.6 fusion.28
  170.7 0.6 reduce_min.9
  172.0 0.0 all-gather.3.cloned.1.call-done
  172.0 121.9 %all-gather.5.cloned.1.call-done = bf16[1536,2048]{1,0:T(8,128)(2,1)} async-done(((bf16[384,2048]{1,0:T(8,128)(2,1)}), bf16[1536,2048]{1,0:T(8,128)(2,1)}) %all-gather.5.cloned.1.call-update) | async-done | bytes 6291472 | tf_op jit(solution)/shard_map/all_gather | solution.py:110
  293.9 57.2 %conditional.1 = (f32[16,384,128]{2,1,0:T(8,128)S(1)}, f32[16,384]{1,0:T(8,128)S(1)}) conditional(s32[]{:T(128)} %convert_element_type.41, () %tuple.16, (s32[1536]{0:T(1024)S(1)}, s32[1536]{0:T(1024)S(1)}, s32[384]{0:T(512)S(1)}, s32[384]{0:T(512)S(1)}, bf16[384,2048]{1,0:T(8,128)(2,1)}, /*index=5*/bf16[1536,2048]{1,0:T(8,128)(2,1)}, ...), branch_computations={%region_5.6_spmd, %region_6.9_spmd} | conditional | flops 4937410560 | bytes 137788496 | solution.py:127
  293.9 0.5 compare_and_fusion
  294.5 0.0 copy-start.2
  294.5 18.5 %select_reduce_fusion = (f32[16,384]{1,0:T(8,128)S(1)}, f32[16,384,1536]{2,1,0:T(8,128)}) fusion(pred[384,1536]{1,0:T(8,128)(4,1)S(1)} %compare_and_fusion, bf16[1536,2048]{1,0:T(8,128)(2,1)} %get-tuple-element.21, bf16[384,2048]{1,0:T(8,128)(2,1)} %get-tuple-element.30), kind=kOutput, calls=%fused_computation.1 | convolution fusion | flops 2444224512 | bytes 46227456 | tf_op jit(solution)/shard_map/cond/branch_1_fun/qhd,khd->hqk/dot_general | solution.py:50
  313.0 21.0 %fusion.2 = f32[16,384,128]{2,1,0:T(8,128)S(1)} fusion(f32[16,384,1536]{2,1,0:T(8,128)} %get-tuple-element.36, f32[16,384]{1,0:T(8,128)S(1)} %broadcast_maximum_fusion, pred[384,1536]{1,0:T(8,128)(4,1)} %copy-done.2, bf16[1536,2048]{1,0:T(8,128)(2,1)} %get-tuple-element.22), kind=kOutput, calls=%fused_computation.4 | convolution fusion | flops 2453667840 | bytes 47800320 | tf_op jit(solution)/shard_map/cond/branch_1_fun/hqk,khd->hqd/dot_general | solution.py:56
  334.0 17.1 %fusion = f32[16,384]{1,0:T(8,128)S(1)} fusion(f32[16,384,1536]{2,1,0:T(8,128)} %get-tuple-element.36, f32[16,384]{1,0:T(8,128)S(1)} %broadcast_maximum_fusion, pred[384,1536]{1,0:T(8,128)(4,1)S(1)} %copy-done.3), kind=kLoop, calls=%fused_computation.2 | loop fusion | flops 37742592 | bytes 38387712 | tf_op jit(solution)/shard_map/cond/branch_1_fun/reduce_sum | solution.py:62
  351.1 1.9 copy_bitcast_fusion.1
  (29 shorter events, 0.1 us)
Async XLA Ops:
  7.2 10.1 %copy-start.11 = (s32[4]{0:T(128)S(1)}, s32[4]{0:T(128)}, u32[]{:S(2)}) copy-start(s32[4]{0:T(128)} %param.17) | copy-start | bytes 52
  7.2 10.2 %copy-start.5 = (bf16[128,128]{1,0:T(8,128)(2,1)S(1)}, bf16[128,128]{1,0:T(8,128)(2,1)}, u32[]{:S(2)}) copy-start(bf16[128,128]{1,0:T(8,128)(2,1)} %param.13) | copy-start | bytes 98308
  7.2 164.8 %all-gather.3.cloned.1.call-start = ((), (), s32[]{:S(2)}) async-start(), calls=%async_computation | async-start | bytes 7864320 | tf_op jit(solution)/shard_map/all_gather | solution.py:109
  7.9 286.0 %all-gather.5.cloned.1.call-start = ((), (), s32[]{:S(2)}) async-start(), calls=%async_computation.1 | async-start | bytes 7864320 | tf_op jit(solution)/shard_map/all_gather | solution.py:110
  10.5 28.9 %copy-start = (bf16[384,2048]{1,0:T(8,128)(2,1)}, bf16[384,2048]{1,0:T(8,128)(2,1)S(1)}, u32[]{:S(2)}) copy-start(bf16[384,2048]{1,0:T(8,128)(2,1)S(1)} %multiply_convert_fusion) | copy-start | bytes 4718596
  11.5 23.4 %collective-permute-start = (bf16[127,2048]{1,0:T(8,128)(2,1)}, bf16[127,2048]{1,0:T(8,128)(2,1)}, u32[]{:S(2)}, u32[]{:S(2)}) collective-permute-start(bf16[127,2048]{1,0:T(8,128)(2,1)} %slice.12), channel_id=1, source_target_pairs={{0,4},{4,8},{8,12},{1,5},{5,9},{9,13},{2,6},{6,10},{10,14},{3,7},{... | collective-permute-start | bytes 1560584 | tf_op jit(solution)/shard_map/ppermute | solution.py:14
  17.2 22.2 %copy-start.6 = (s32[384]{0:T(512)}, s32[384]{0:T(512)S(1)}, u32[]{:S(2)}) copy-start(s32[384]{0:T(512)S(1)} %iota_add_fusion.1) | copy-start | bytes 4612
  148.5 13.9 %copy-start.1 = (bf16[384,2048]{1,0:T(8,128)(2,1)S(1)}, bf16[384,2048]{1,0:T(8,128)(2,1)}, u32[]{:S(2)}) copy-start(bf16[384,2048]{1,0:T(8,128)(2,1)} %copy-done) | copy-start | bytes 4718596
  148.5 13.9 %copy-start.4 = (bf16[384,2048]{1,0:T(8,128)(2,1)S(1)}, bf16[384,2048]{1,0:T(8,128)(2,1)}, u32[]{:S(2)}) copy-start(bf16[384,2048]{1,0:T(8,128)(2,1)} %param.10) | copy-start | bytes 4718596
  148.5 13.9 %copy-start.9 = (f32[2048]{0:T(1024)S(1)}, f32[2048]{0:T(1024)}, u32[]{:S(2)}) copy-start(f32[2048]{0:T(1024)} %param.14) | copy-start | bytes 24580
  148.5 13.9 %copy-start.10 = (pred[384]{0:T(512)(128)(4,1)S(1)}, pred[384]{0:T(512)(128)(4,1)}, u32[]{:S(2)}) copy-start(pred[384]{0:T(512)(128)(4,1)} %fusion.26) | copy-start | bytes 1156
  162.5 8.2 %copy-start.8 = (s32[384]{0:T(512)S(1)}, s32[384]{0:T(512)}, u32[]{:S(2)}) copy-start(s32[384]{0:T(512)} %get-tuple-element.31) | copy-start | bytes 4612
  162.5 131.5 %copy-start.7 = (s32[384]{0:T(512)S(1)}, s32[384]{0:T(512)}, u32[]{:S(2)}) copy-start(s32[384]{0:T(512)} %copy-done.6) | copy-start | bytes 4612
  294.5 18.5 %copy-start.2 = (pred[384,1536]{1,0:T(8,128)(4,1)}, pred[384,1536]{1,0:T(8,128)(4,1)S(1)}, u32[]{:S(2)}) copy-start(pred[384,1536]{1,0:T(8,128)(4,1)S(1)} %compare_and_fusion) | copy-start | bytes 1769476 | tf_op jit(solution)/shard_map/cond
  313.0 21.0 %copy-start.3 = (pred[384,1536]{1,0:T(8,128)(4,1)S(1)}, pred[384,1536]{1,0:T(8,128)(4,1)}, u32[]{:S(2)}) copy-start(pred[384,1536]{1,0:T(8,128)(4,1)} %copy-done.2) | copy-start | bytes 1769476 | tf_op jit(solution)/shard_map/cond
Sparse Core Ops, SparseCore 0:
  9.6 119.8 all-gather.2
  169.5 124.3 all-gather.4
where the time goes:
time: 360 us
  waiting for transfers between devices  136 us (38%)
  matrix products  130 us (36%)
  other arithmetic  49.8 us (14%)
  local copies, waits for them, and re-layouts  21.9 us (6%)
  between operations  15.5 us (4%)
  starting transfers between devices  5.79 us (2%)
    all_gather x1, waiting for transfers between devices, per_device(): values_piece = lax.all_gather(hyena_mix, 'ctx', axis=0, tiled=True)  122 us
    conv_general_dilated x1, matrix products, grouped_filter(): lax.conv_general_dilated(stacked, kernel, (1,), [(left_pad, 0)], dimensio...  90.8 us
    dot_general x1, matrix products, attend_update(): jnp.einsum('hqk,khd->hqd', weights.astype(jnp.bfloat16), value_heads, pre...  21 us
    dot_general x1, matrix products, attend_update(): jnp.einsum('qhd,khd->hqk', queries, key_heads, preferred_element_type=jnp...  18.5 us
    reduce_sum x1, other arithmetic, attend_update(): return (mixed, new_max, jnp.sum(weights, axis=2))  17.1 us
    slice x1, local copies, waits for them, and re-layouts, per_device(): both_parities[1]  13.9 us
    ppermute x1, waiting for transfers between devices, passed_along(): return lax.ppermute(value, axis, pairs)  13.9 us
    conv_general_dilated x1, other arithmetic, grouped_filter(): lax.conv_general_dilated(stacked, kernel, (1,), [(left_pad, 0)], dimensio...  9.64 us
  transfers between devices with their start and end apart: 3, of which 2 were waited for; matrix products, arithmetic and copies ran while one was open for 40% of the time, Pallas kernels for 0%

commit v1 on v0

--- a/solution.py
+++ b/solution.py
@@ -106,8 +106,11 @@
         )
     )
     offset_row = jnp.int32(0)
-    keys_piece = lax.all_gather(attn_key, "ctx", axis=0, tiled=True)
-    values_piece = lax.all_gather(hyena_mix, "ctx", axis=0, tiled=True)
+    keys_piece, values_piece = jnp.split(
+        lax.all_gather(jnp.concatenate([attn_key, hyena_mix], axis=1), "ctx", axis=0, tiled=True),
+        [attn_key.shape[1]],
+        axis=1,
+    )
     key_rows = keys_piece.shape[0]
     key_heads = keys_piece.reshape(key_rows, head_count, HEAD_DIM)
     value_heads = values_piece.reshape(key_rows, head_count, HEAD_DIM)

time: 360 us -> 473 us (1.31)
  waiting for transfers between devices: 136 us -> 225 us
  local copies, waits for them, and re-layouts: 21.9 us -> 50 us
    all_gather x2 -> x1, waiting for transfers between devices: 122 us -> 219 us  [per_device(): lax.all_gather(jnp.concatenate([attn_key, hyena_mix], axis=1), 'ctx', axi...]
    another operation x0 -> x1, local copies, waits for them, and re-layouts: none -> 16.7 us
    split x0 -> x1, local copies, waits for them, and re-layouts: none -> 10.3 us  [per_device(): jnp.split(lax.all_gather(jnp.concatenate([attn_key, hyena_mix], axis=1),...]
    ppermute x1, waiting for transfers between devices: 13.9 us -> 6.22 us  [passed_along(): return lax.ppermute(value, axis, pairs)]
  transfers between devices with their start and end apart: 3 -> 2, of which waited for: 2 -> 2; matrix products, arithmetic and copies ran while one was open for 40% -> 1% of each run, Pallas kernels for 0% -> 0%
where the time goes in v1:
time: 473 us
  waiting for transfers between devices  225 us (48%)
  matrix products  126 us (27%)
  other arithmetic  50.8 us (11%)
  local copies, waits for them, and re-layouts  50 us (11%)
  between operations  15.4 us (3%)
  starting transfers between devices  5.76 us (1%)
    all_gather x1, waiting for transfers between devices, per_device(): lax.all_gather(jnp.concatenate([attn_key, hyena_mix], axis=1), 'ctx', axi...  219 us
    conv_general_dilated x1, matrix products, grouped_filter(): lax.conv_general_dilated(stacked, kernel, (1,), [(left_pad, 0)], dimensio...  90.8 us
    dot_general x1, matrix products, attend_update(): jnp.einsum('qhd,khd->hqk', queries, key_heads, preferred_element_type=jnp...  18 us
    reduce_sum x1, other arithmetic, attend_update(): return (mixed, new_max, jnp.sum(weights, axis=2))  17.2 us
    dot_general x1, matrix products, attend_update(): jnp.einsum('hqk,khd->hqd', weights.astype(jnp.bfloat16), value_heads, pre...  17.1 us
    another operation x1, local copies, waits for them, and re-layouts  16.7 us
    slice x1, local copies, waits for them, and re-layouts, per_device(): both_parities[1]  13.9 us
    split x1, local copies, waits for them, and re-layouts, per_device(): jnp.split(lax.all_gather(jnp.concatenate([attn_key, hyena_mix], axis=1),...  10.3 us
  transfers between devices with their start and end apart: 2, of which 2 were waited for; matrix products, arithmetic and copies ran while one was open for 1% of the time, Pallas kernels for 0%

profile of v1, /device:TPU:0, one launch (start us, length us, event | category | flops | bytes accessed | tf_op | source)
XLA Modules:
  0.0 472.8 jit_solution(14397683990399156630)
XLA Ops:
  7.2 0.0 all-gather.2.cloned.1.call-start
  7.2 2.5 multiply_convert_fusion
  9.7 1.0 slice.12
  10.8 5.7 %collective-permute-start = (bf16[127,2048]{1,0:T(8,128)(2,1)}, bf16[127,2048]{1,0:T(8,128)(2,1)}, u32[]{:S(2)}, u32[]{:S(2)}) collective-permute-start(bf16[127,2048]{1,0:T(8,128)(2,1)} %slice.12), channel_id=1, source_target_pairs={{0,4},{4,8},{8,12},{1,5},{5,9},{9,13},{2,6},{6,10},{10,14},{3,7},{... | collective-permute-start | bytes 1560584 | tf_op jit(solution)/shard_map/ppermute | solution.py:14
  16.5 0.6 iota_add_fusion.1
  17.1 0.1 convert_reduce_fusion
  17.2 0.1 broadcast_in_dim.88
  17.3 1.5 rev.3
  18.8 0.9 copy.43
  19.7 0.7 fusion.20
  20.4 0.5 fusion.22
  20.9 6.2 %collective-permute-done = bf16[127,2048]{1,0:T(8,128)(2,1)} collective-permute-done((bf16[127,2048]{1,0:T(8,128)(2,1)}, bf16[127,2048]{1,0:T(8,128)(2,1)}, u32[]{:S(2)}, u32[]{:S(2)}) %collective-permute-start) | collective-permute-done | bytes 520224 | tf_op jit(solution)/shard_map/ppermute | solution.py:14
  27.2 1.8 copy_dynamic-update-slice_fusion.1
  29.0 2.6 copy_dynamic-update-slice_fusion
  31.6 8.6 %broadcast_select_fusion.1 = (bf16[1,511,2048]{2,0,1:T(2,128)(2,1)S(1)}, bf16[1,511,2048]{2,0,1:T(2,128)(2,1)S(1)}) fusion(bf16[1,511,2048]{2,0,1:T(2,128)(2,1)S(1)} %copy_dynamic-update-slice_fusion, pred[511]{0:T(512)(128)(4,1)S(1)} %get-tuple-element.51, pred[511]{0:T(512)(128)(4,1)S(1)} %broadcast_compare_fusion), kind=kLoop, calls=%fused_computation.14 | loop fusion | flops 2093056 | bytes 6280190 | tf_op jit(solution)/shard_map/jit(_where)/select_n | solution.py:32
  40.3 9.6 %fusion.36 = bf16[2,511,2048]{2,0,1:T(2,128)(2,1)S(1)} fusion(bf16[1,511,2048]{2,0,1:T(2,128)(2,1)S(1)} %get-tuple-element.60, bf16[1,511,2048]{2,0,1:T(2,128)(2,1)S(1)} %get-tuple-element.59), kind=kLoop, calls=%fused_computation.16.clone.1 | loop fusion | flops 8372224 | bytes 8372224 | tf_op jit(solution)/shard_map/conv_general_dilated | solution.py:35
  49.9 90.8 %fusion.10 = f32[2,384,2048]{2,0,1:T(2,128)} fusion(bf16[128,1,2048]{2,1,0:T(2,128)(2,1)S(1)} %copy.43, bf16[2,511,2048]{2,0,1:T(2,128)(2,1)S(1)} %fusion.36), kind=kOutput, calls=%fused_computation.15 | convolution fusion | flops 402653184 | bytes 11001856 | tf_op jit(solution)/shard_map/conv_general_dilated | solution.py:35
  140.8 13.9 %fusion.27 = (f32[1,384,2048]{2,0,1:T(1,128)}, f32[1,384,2048]{2,0,1:T(1,128)}) fusion(f32[2,384,2048]{2,0,1:T(2,128)} %fusion.10), kind=kLoop, calls=%fused_computation.52 | loop fusion | bytes 12582912 | tf_op jit(solution)/shard_map/slice | solution.py:86
  154.7 5.9 %fusion.17 = bf16[384,2048]{1,0:T(8,128)(2,1)S(1)} fusion(f32[1,384,2048]{2,0,1:T(1,128)} %get-tuple-element.58, f32[1,384,2048]{2,0,1:T(1,128)} %get-tuple-element.57, bf16[384,2048]{1,0:T(8,128)(2,1)S(1)} %copy-done.1, bf16[384,2048]{1,0:T(8,128)(2,1)S(1)} %copy-done.5, f32[2048]{0:T(1024)S(1)} %copy-done.11, pred[384]{0:T(512)(128)(4,1)S(1)} %copy-done.12), kind=kLoop, calls=%fused_computation.24 | loop fusion | flops 5505024 | bytes 11018624 | tf_op jit(solution)/shard_map/convert_element_type | solution.py:90
  160.6 1.1 copy-done.3
  161.7 2.0 pad_maximum_fusion
  163.7 0.0 all-gather.2.cloned.1.call-update
  164.3 0.6 reduce_min.9
  165.6 218.7 %all-gather.2.cloned.1.call-done = bf16[1536,4096]{1,0:T(8,128)(2,1)} async-done(((bf16[384,4096]{1,0:T(8,128)(2,1)}), bf16[1536,4096]{1,0:T(8,128)(2,1)}) %all-gather.2.cloned.1.call-update) | async-done | bytes 12582928 | tf_op jit(solution)/shard_map/all_gather | solution.py:110
  384.3 79.8 %conditional.1 = (f32[16,384,128]{2,1,0:T(8,128)S(1)}, f32[16,384]{1,0:T(8,128)S(1)}) conditional(s32[]{:T(128)} %convert_element_type.41, () %tuple.16, (s32[1536]{0:T(1024)S(1)}, s32[1536]{0:T(1024)S(1)}, s32[384]{0:T(512)S(1)}, s32[384]{0:T(512)S(1)}, bf16[384,2048]{1,0:T(8,128)(2,1)}, /*index=5*/bf16[1536,4096]{1,0:T(8,128)(2,1)}) %tuple.34), branch_computations={%region_5.6_spmd, %region_6.9_spmd} | conditional | flops 4937410560 | bytes 192052304 | solution.py:130
  384.3 16.7 %copy.45 = bf16[1536,4096]{0,1:T(8,128)(2,1)} copy(bf16[1536,4096]{1,0:T(8,128)(2,1)} %get-tuple-element.48) | data formatting | bytes 25165824 | tf_op jit(solution)/shard_map
  400.9 10.3 %fusion.26 = (bf16[1536,2048]{0,1:T(8,128)(2,1)}, bf16[1536,2048]{0,1:T(8,128)(2,1)}) fusion(bf16[1536,4096]{0,1:T(8,128)(2,1)} %copy.45), kind=kLoop, calls=%fused_computation.51 | loop fusion | bytes 25165824 | tf_op jit(solution)/shard_map/split | solution.py:109
  411.2 0.5 compare_and_fusion
  411.8 18.0 %select_reduce_fusion = (f32[16,384]{1,0:T(8,128)S(1)}, f32[16,384,1536]{2,1,0:T(8,128)}) fusion(pred[384,1536]{1,0:T(8,128)(4,1)S(1)} %compare_and_fusion, bf16[1536,16,128]{0,2,1:T(8,128)(2,1)} %bitcast.40, bf16[384,2048]{1,0:T(8,128)(2,1)S(1)} %copy-done.4), kind=kOutput, calls=%fused_computation.1 | convolution fusion | flops 2444224512 | bytes 46227456 | tf_op jit(solution)/shard_map/cond/branch_1_fun/qhd,khd->hqk/dot_general | solution.py:50
  429.8 17.1 %fusion.2 = f32[16,384,128]{2,1,0:T(8,128)S(1)} fusion(bf16[1536,16,128]{0,2,1:T(8,128)(2,1)} %bitcast.42, f32[16,384,1536]{2,1,0:T(8,128)} %get-tuple-element.56, f32[16,384]{1,0:T(8,128)S(1)} %broadcast_maximum_fusion, pred[384,1536]{1,0:T(8,128)(4,1)} %copy-done.2), kind=kOutput, calls=%fused_computation.4 | convolution fusion | flops 2453667840 | bytes 47800320 | tf_op jit(solution)/shard_map/cond/branch_1_fun/hqk,khd->hqd/dot_general | solution.py:56
  446.9 17.2 %fusion = f32[16,384]{1,0:T(8,128)S(1)} fusion(f32[16,384,1536]{2,1,0:T(8,128)} %get-tuple-element.56, f32[16,384]{1,0:T(8,128)S(1)} %broadcast_maximum_fusion, pred[384,1536]{1,0:T(8,128)(4,1)} %copy-done.2), kind=kLoop, calls=%fused_computation.2 | loop fusion | flops 37742592 | bytes 38387712 | tf_op jit(solution)/shard_map/cond/branch_1_fun/reduce_sum | solution.py:62
  464.1 1.9 copy_bitcast_fusion.1
  (32 shorter events, 0.1 us)
Async XLA Ops:
  7.2 9.9 %copy-start.13 = (s32[4]{0:T(128)S(1)}, s32[4]{0:T(128)}, u32[]{:S(2)}) copy-start(s32[4]{0:T(128)} %param.17) | copy-start | bytes 52
  7.2 10.0 %copy-start.7 = (bf16[128,128]{1,0:T(8,128)(2,1)S(1)}, bf16[128,128]{1,0:T(8,128)(2,1)}, u32[]{:S(2)}) copy-start(bf16[128,128]{1,0:T(8,128)(2,1)} %param.13) | copy-start | bytes 98308
  7.2 377.1 %all-gather.2.cloned.1.call-start = ((), (), s32[]{:S(2)}) async-start(), calls=%async_computation | async-start | bytes 15728640 | tf_op jit(solution)/shard_map/all_gather | solution.py:110
  9.7 21.9 %copy-start = (bf16[384,2048]{1,0:T(8,128)(2,1)}, bf16[384,2048]{1,0:T(8,128)(2,1)S(1)}, u32[]{:S(2)}) copy-start(bf16[384,2048]{1,0:T(8,128)(2,1)S(1)} %multiply_convert_fusion) | copy-start | bytes 4718596
  10.8 16.4 %collective-permute-start = (bf16[127,2048]{1,0:T(8,128)(2,1)}, bf16[127,2048]{1,0:T(8,128)(2,1)}, u32[]{:S(2)}, u32[]{:S(2)}) collective-permute-start(bf16[127,2048]{1,0:T(8,128)(2,1)} %slice.12), channel_id=1, source_target_pairs={{0,4},{4,8},{8,12},{1,5},{5,9},{9,13},{2,6},{6,10},{10,14},{3,7},{... | collective-permute-start | bytes 1560584 | tf_op jit(solution)/shard_map/ppermute | solution.py:14
  17.1 14.5 %copy-start.8 = (s32[384]{0:T(512)}, s32[384]{0:T(512)S(1)}, u32[]{:S(2)}) copy-start(s32[384]{0:T(512)S(1)} %get-tuple-element.61) | copy-start | bytes 4612
  140.8 13.9 %copy-start.1 = (bf16[384,2048]{1,0:T(8,128)(2,1)S(1)}, bf16[384,2048]{1,0:T(8,128)(2,1)}, u32[]{:S(2)}) copy-start(bf16[384,2048]{1,0:T(8,128)(2,1)} %copy-done) | copy-start | bytes 4718596
  140.8 13.9 %copy-start.5 = (bf16[384,2048]{1,0:T(8,128)(2,1)S(1)}, bf16[384,2048]{1,0:T(8,128)(2,1)}, u32[]{:S(2)}) copy-start(bf16[384,2048]{1,0:T(8,128)(2,1)} %param.10) | copy-start | bytes 4718596
  140.8 13.9 %copy-start.11 = (f32[2048]{0:T(1024)S(1)}, f32[2048]{0:T(1024)}, u32[]{:S(2)}) copy-start(f32[2048]{0:T(1024)} %param.14) | copy-start | bytes 24580
  140.8 13.9 %copy-start.12 = (pred[384]{0:T(512)(128)(4,1)S(1)}, pred[384]{0:T(512)(128)(4,1)}, u32[]{:S(2)}) copy-start(pred[384]{0:T(512)(128)(4,1)} %fusion.22) | copy-start | bytes 1156
  154.7 7.0 %copy-start.6 = (bf16[384,2048]{1,0:T(8,128)(2,1)S(1)}, bf16[384,2048]{1,0:T(8,128)(2,1)}, u32[]{:S(2)}) copy-start(bf16[384,2048]{1,0:T(8,128)(2,1)} %param.16) | copy-start | bytes 4718596
  160.6 1.1 copy-start.3
  161.7 2.6 copy-start.10
  161.7 222.6 %copy-start.9 = (s32[384]{0:T(512)S(1)}, s32[384]{0:T(512)}, u32[]{:S(2)}) copy-start(s32[384]{0:T(512)} %copy-done.8) | copy-start | bytes 4612
  400.9 10.8 %copy-start.4 = (bf16[384,2048]{1,0:T(8,128)(2,1)S(1)}, bf16[384,2048]{1,0:T(8,128)(2,1)}, u32[]{:S(2)}) copy-start(bf16[384,2048]{1,0:T(8,128)(2,1)} %get-tuple-element.30) | copy-start | bytes 4718596 | tf_op jit(solution)/shard_map/cond
  411.8 18.0 %copy-start.2 = (pred[384,1536]{1,0:T(8,128)(4,1)}, pred[384,1536]{1,0:T(8,128)(4,1)S(1)}, u32[]{:S(2)}) copy-start(pred[384,1536]{1,0:T(8,128)(4,1)S(1)} %compare_and_fusion) | copy-start | bytes 1769476 | tf_op jit(solution)/shard_map/cond
Sparse Core Ops, SparseCore 0:
  163.9 220.3 all-gather.1
